TPU v7x, 256 devices: a whole 4x4x8 slice. The times are simulated.
256 devices in a mesh: dp: 64 (over x, z, core), rep: 4 (over y).
Axes of the slice: x: 4, y: 4, z: 8, core: 2. Of those that a mesh axis runs over, the one named last changes fastest.
Arguments:
- frames_in: bfloat16 [4, 57344, 1536], P('rep', 'dp')
- lengths: int32 [4, 64, 4], P('rep', 'dp'), may hold values from 1 to 893, as said below
- norm_gain: float32 [1536], replicated, may hold values from 0.5 to 1.5
- norm_bias: float32 [1536], replicated, may hold values from -2 to 2
- w_in: bfloat16 [1536, 3072], P(('dp', 'rep')), may hold values from -0.15625 to 0.15625
- kernel: float32 [31, 1536], replicated, may hold values from -1 to 1
- batch_gain: float32 [1536], replicated, may hold values from 0.5 to 1.5
- batch_bias: float32 [1536], replicated, may hold values from -3 to 3
- w_out: bfloat16 [1536, 1536], P(('dp', 'rep')), may hold values from -0.15625 to 0.15625
Outputs:
- frames_out: bfloat16 [4, 57344, 1536], P('rep', 'dp')
Inputs may be any that keep to these rules, and one draw needn't show every extreme that they name: `lengths`: for each rep index, the devices 2k and 2k + 1 of dp hold 1024 frames together, so each rep index holds 512 frames for each of its dp devices; a device holds at most 896 frames, and some device of every rep index holds exactly 896.
All inputs are finite; a program needn't handle non-finite values.
Results may differ from a plain program's by a relative error of at most 0.0038.
Values may be sent and summed in bfloat16 or wider, within the bound.
A program may use at most 128 MiB of HBM per device.

v0:
```python
import jax
import jax.numpy as jnp
from jax import lax
from jax.sharding import PartitionSpec as P

FR_DEV = 512
EPSILON = 1e-05


def layer_norm(frames, norm_gain, norm_bias):
    values = frames.astype(jnp.float32)
    average = jnp.mean(values, axis=-1, keepdims=True)
    centred = values - average
    spread = jnp.mean(centred * centred, axis=-1, keepdims=True)
    return centred * lax.rsqrt(spread + EPSILON) * norm_gain + norm_bias


def depthwise(gated, labels, kernel):
    half_kernel = kernel.shape[0] // 2
    length_rows = gated.shape[0]
    padded = jnp.pad(gated, ((half_kernel, half_kernel), (0, 0)))
    padded_labels = jnp.pad(labels, (half_kernel, half_kernel), constant_values=-1)
    summed = jnp.zeros(gated.shape, jnp.float32)
    for offset in range(kernel.shape[0]):
        shared = padded_labels[offset : offset + length_rows] == labels
        contribution = jnp.where(
            shared[:, None], padded[offset : offset + length_rows].astype(jnp.float32), 0.0
        )
        summed = summed + contribution * kernel[offset]
    return summed


def project_in(normed, weight_rows):
    return jnp.dot(normed, weight_rows, preferred_element_type=jnp.float32)


def project_out(active, weight_rows):
    return jnp.dot(active, weight_rows, preferred_element_type=jnp.float32)


def on_device(
    frames_in, lengths, norm_gain, norm_bias, w_in, kernel, batch_gain, batch_bias, w_out
):
    local_frames = frames_in[0]
    local_lengths = lengths[0, 0]
    capacity = local_frames.shape[0]
    features = local_frames.shape[1]
    total_count = lax.axis_size("dp") * lax.axis_size("rep") * FR_DEV
    grouped = (w_in, w_out)
    grouped = (
        lax.all_gather(w_in, ("dp", "rep"), axis=0, tiled=True),
        lax.all_gather(w_out, ("dp", "rep"), axis=0, tiled=True),
    )
    rows_here = jnp.arange(capacity, dtype=jnp.int32)
    local_load = jnp.sum(local_lengths)
    bounds = jnp.cumsum(local_lengths)
    labels = jnp.sum((rows_here[:, None] >= bounds[None, :]).astype(jnp.int32), axis=1)
    row_weight = (rows_here < local_load).astype(jnp.float32)[:, None]
    normed = layer_norm(local_frames, norm_gain, norm_bias).astype(jnp.bfloat16)
    projected = project_in(normed, grouped[0])
    gated = (projected[:, :features] * jax.nn.sigmoid(projected[:, features:])).astype(jnp.bfloat16)
    convolved = depthwise(gated, labels, kernel)
    average = lax.psum(jnp.sum(convolved * row_weight, axis=0), ("dp", "rep")) / total_count
    centred = convolved - average
    spread = lax.psum(jnp.sum(centred * centred * row_weight, axis=0), ("dp", "rep")) / total_count
    scaled = centred * lax.rsqrt(spread + EPSILON) * batch_gain + batch_bias
    active = jax.nn.silu(scaled).astype(jnp.bfloat16)
    branch = project_out(active, grouped[1])
    mixed = (local_frames.astype(jnp.float32) + branch).astype(jnp.bfloat16)
    result = jnp.where(rows_here[:, None] < local_load, mixed, jnp.zeros_like(mixed))
    return result[None]


def solution(mesh):
    placed = (
        P("rep", "dp", None),
        P("rep", "dp", None),
        P(),
        P(),
        P(("dp", "rep"), None),
        P(),
        P(),
        P(),
        P(("dp", "rep"), None),
    )
    return jax.shard_map(
        on_device, mesh=mesh, in_specs=placed, out_specs=P("rep", "dp", None), check_vma=False
    )
```

profile of v0, /device:TPU:1, one launch (start us, length us, event | category | flops | bytes accessed | tf_op | source)
XLA Modules:
  0.0 487.7 jit_solution(4124133330554323458)
XLA Ops:
  6.5 0.7 all-gather.7.cloned.1.call-update
  7.3 0.7 all-gather.5.cloned.1.call-update
  8.0 1.3 reduce_sum.54
  9.3 0.8 reduce-window.8
  10.1 0.6 iota_compare_fusion.1
  10.8 0.7 fusion.26
  11.5 1.5 slice_reduce_fusion.29
  13.0 1.8 slice_reduce_fusion.30
  14.9 2.2 convert_reduce_fusion
  17.2 2.6 fusion.4
  19.8 0.1 slice_compare_fusion.29
  19.9 0.1 slice_compare_fusion.28
  20.0 0.1 slice_compare_fusion.27
  20.1 111.2 %all-gather.7.cloned.1.call-done = bf16[256,6,1536]{2,1,0:T(8,128)(2,1)} async-done(((bf16[1,6,1536]{2,1,0:T(8,128)(2,1)}), bf16[256,6,1536]{2,1,0:T(8,128)(2,1)}) %all-gather.7.cloned.1.call-update) | async-done | bytes 4718608 | tf_op jit(solution)/shard_map/all_gather | solution.py:52
  131.3 8.5 %reshape.87 = bf16[1536,1536]{1,0:T(8,128)(2,1)} reshape(bf16[256,6,1536]{2,1,0:T(8,128)(2,1)} %all-gather.7.cloned.1.call-done) | data formatting | bytes 9437184
  139.8 113.5 %all-gather.5.cloned.1.call-done = bf16[256,6,3072]{2,1,0:T(8,128)(2,1)} async-done(((bf16[1,6,3072]{2,1,0:T(8,128)(2,1)}), bf16[256,6,3072]{2,1,0:T(8,128)(2,1)}) %all-gather.5.cloned.1.call-update) | async-done | bytes 9437200 | tf_op jit(solution)/shard_map/all_gather | solution.py:51
  253.3 14.2 %reshape.85 = bf16[1536,3072]{1,0:T(8,128)(2,1)} reshape(bf16[256,6,3072]{2,1,0:T(8,128)(2,1)} %all-gather.5.cloned.1.call-done) | data formatting | bytes 18874368
  267.5 11.3 %fusion.16 = f32[896,3072]{1,0:T(8,128)S(1)} fusion(bf16[1536,3072]{1,0:T(8,128)(2,1)} %reshape.85, bf16[1,896,1536]{2,1,0:T(8,128)(2,1)S(1)} %copy-done, f32[1536]{0:T(1024)S(1)} %copy-done.2, f32[1536]{0:T(1024)S(1)} %copy-done.3, f32[896]{0:T(1024)S(1)} %add_rsqrt_fusion.1, f32[896]{0:T(1024)S(1)} %broadcast_multiply_fusion.1), kind=kOutput, calls=%fused_computation.23 | convolution fusion | flops 8463974400 | bytes 23219200 | tf_op jit(solution)/shard_map/dot_general | solution.py:34
  278.8 1.5 fusion.13
  280.4 38.3 %multiply_reduce_fusion.1 = (f32[1536]{0:T(1024)S(1)}, f32[896,1536]{1,0:T(8,128)}) fusion(f32[896]{0:T(1024)S(1)} %fusion.26, f32[1536]{0:T(1024)S(1)} %get-tuple-element.34, pred[896]{0:T(1024)(128)(4,1)S(1)} %get-tuple-element.67, f32[1536]{0:T(1024)S(1)} %get-tuple-element.35, pred[896]{0:T(1024)(128)(4,1)S(1)} %get-tuple-element.39, ...), kind=kLoop, calls=%fused_computation.18 | loop fusion | flops 170654208 | bytes 8484608 | tf_op jit(solution)/shard_map/reduce_sum | solution.py:63
  318.7 74.8 %psum.14 = f32[1536]{0:T(1024)S(1)} all-reduce(f32[1536]{0:T(1024)S(1)} %get-tuple-element.36), channel_id=1, replica_groups=mesh['dp'=64,'rep'=4] {'dp','rep'}, use_global_device_ids=true, to_apply=%region_6.7 | all-reduce | flops 1536 | bytes 12288 | tf_op jit(solution)/shard_map/psum | solution.py:63
  393.5 3.3 multiply_reduce_fusion
  396.8 73.6 %psum.15 = f32[1536]{0:T(1024)S(1)} all-reduce(f32[1536]{0:T(1024)S(1)} %multiply_reduce_fusion), channel_id=1, replica_groups=mesh['dp'=64,'rep'=4] {'dp','rep'}, use_global_device_ids=true, to_apply=%region_8.9 | all-reduce | flops 1536 | bytes 12288 | tf_op jit(solution)/shard_map/psum | solution.py:65
  470.4 10.4 %fusion.15 = bf16[1,896,1536]{2,1,0:T(8,128)(2,1)} fusion(bf16[1536,1536]{1,0:T(8,128)(2,1)} %reshape.87, bf16[1,896,1536]{2,1,0:T(8,128)(2,1)S(1)} %copy-done.1, f32[896,1536]{1,0:T(8,128)} %get-tuple-element.37, f32[1536]{0:T(1024)S(1)} %copy-done.4, f32[1536]{0:T(1024)S(1)} %copy-done.5, f32[1536]{0:T(1024)S(1)} %add_rsqrt_fusion, ...), kind=kOutput, calls=%fused_computation.22 | convolution fusion | flops 4245749760 | bytes 15754112 | tf_op jit(solution)/shard_map/dot_general | solution.py:38
  (20 shorter events, 0.2 us)
Async XLA Ops:
  6.5 124.8 %all-gather.7.cloned.1.call-start = ((), (), s32[]{:S(2)}) async-start(), calls=%async_computation.1 | async-start | bytes 6316032 | tf_op jit(solution)/shard_map/all_gather | solution.py:52
  7.3 246.1 %all-gather.5.cloned.1.call-start = ((), (), s32[]{:S(2)}) async-start(), calls=%async_computation | async-start | bytes 12632064 | tf_op jit(solution)/shard_map/all_gather | solution.py:51
  139.8 127.7 %copy-start = (bf16[1,896,1536]{2,1,0:T(8,128)(2,1)S(1)}, bf16[1,896,1536]{2,1,0:T(8,128)(2,1)}, u32[]{:S(2)}) copy-start(bf16[1,896,1536]{2,1,0:T(8,128)(2,1)} %param.9) | copy-start | bytes 8257540
  139.8 127.7 %copy-start.2 = (f32[1536]{0:T(1024)S(1)}, f32[1536]{0:T(1024)}, u32[]{:S(2)}) copy-start(f32[1536]{0:T(1024)} %param.12) | copy-start | bytes 18436
  139.8 127.7 %copy-start.3 = (f32[1536]{0:T(1024)S(1)}, f32[1536]{0:T(1024)}, u32[]{:S(2)}) copy-start(f32[1536]{0:T(1024)} %param.11) | copy-start | bytes 18436
  280.4 190.1 %copy-start.4 = (f32[1536]{0:T(1024)S(1)}, f32[1536]{0:T(1024)}, u32[]{:S(2)}) copy-start(f32[1536]{0:T(1024)} %param.16) | copy-start | bytes 18436
  280.4 190.1 %copy-start.5 = (f32[1536]{0:T(1024)S(1)}, f32[1536]{0:T(1024)}, u32[]{:S(2)}) copy-start(f32[1536]{0:T(1024)} %param.15) | copy-start | bytes 18436
  318.7 151.7 %copy-start.1 = (bf16[1,896,1536]{2,1,0:T(8,128)(2,1)S(1)}, bf16[1,896,1536]{2,1,0:T(8,128)(2,1)}, u32[]{:S(2)}) copy-start(bf16[1,896,1536]{2,1,0:T(8,128)(2,1)} %param.9) | copy-start | bytes 8257540
Sparse Core Ops, SparseCore 0:
  11.2 120.0 all-gather.6
  135.1 118.1 all-gather.4
where the time goes:
time: 489 us; the launch traced here: 488 us
  waiting for transfers between devices  226 us (46%)
  blocking collectives  148 us (30%)
  other arithmetic  51.8 us (11%)
  local copies, waits for them, and re-layouts  26 us (5%)
  matrix products  21.8 us (4%)
  between operations  13.5 us (3%)
    all_gather x1, waiting for transfers between devices, on_device(): lax.all_gather(w_in, ('dp', 'rep'), axis=0, tiled=True)  114 us
    all_gather x1, waiting for transfers between devices, on_device(): lax.all_gather(w_out, ('dp', 'rep'), axis=0, tiled=True)  111 us
    psum x1, blocking collectives, on_device(): lax.psum(jnp.sum(convolved * row_weight, axis=0), ('dp', 'rep'))  74.8 us
    psum x1, blocking collectives, on_device(): lax.psum(jnp.sum(centred * centred * row_weight, axis=0), ('dp', 'rep'))  73.6 us
    reduce_sum x1, other arithmetic, on_device(): jnp.sum(convolved * row_weight, axis=0)  38.3 us
    unnamed x14, local copies, waits for them, and re-layouts  22.6 us
    dot_general x1, matrix products, project_in(): return jnp.dot(normed, weight_rows, preferred_element_type=jnp.float32)  11.3 us
    dot_general x1, matrix products, project_out(): return jnp.dot(active, weight_rows, preferred_element_type=jnp.float32)  10.4 us
  transfers between devices with their start and end apart: 2, of which 2 were waited for; matrix products, arithmetic and copies ran while one was open for 4% of the time, Pallas kernels for 0%

commit v1 on v0

--- a/solution.py
+++ b/solution.py
@@ -41,6 +41,11 @@
 def on_device(
     frames_in, lengths, norm_gain, norm_bias, w_in, kernel, batch_gain, batch_bias, w_out
 ):
+
+    def keep_up_squares_by_axis(own_rows, across, axis_tag):
+        a_now = lax.psum(lax.psum(own_rows, axis_name=across), axis_name=axis_tag)
+        return a_now
+
     local_frames = frames_in[0]
     local_lengths = lengths[0, 0]
     capacity = local_frames.shape[0]
@@ -60,7 +65,9 @@
     projected = project_in(normed, grouped[0])
     gated = (projected[:, :features] * jax.nn.sigmoid(projected[:, features:])).astype(jnp.bfloat16)
     convolved = depthwise(gated, labels, kernel)
-    average = lax.psum(jnp.sum(convolved * row_weight, axis=0), ("dp", "rep")) / total_count
+    average = (
+        keep_up_squares_by_axis(jnp.sum(convolved * row_weight, axis=0), "rep", "dp") / total_count
+    )
     centred = convolved - average
     spread = lax.psum(jnp.sum(centred * centred * row_weight, axis=0), ("dp", "rep")) / total_count
     scaled = centred * lax.rsqrt(spread + EPSILON) * batch_gain + batch_bias

time: 489 us -> 550 us (1.12)
  blocking collectives: 148 us -> 209 us
    psum x1 -> x2, blocking collectives: 74.8 us -> 136 us  [keep_up_squares_by_axis(): a_now = lax.psum(lax.psum(own_rows, axis_name=across), axis_name=axis_tag)]
where the time goes in v1:
time: 550 us; the launch traced here: 549 us
  waiting for transfers between devices  226 us (41%)
  blocking collectives  209 us (38%)
  other arithmetic  51.8 us (9%)
  local copies, waits for them, and re-layouts  26 us (5%)
  matrix products  21.8 us (4%)
  between operations  13.5 us (2%)
    psum x2, blocking collectives, keep_up_squares_by_axis(): a_now = lax.psum(lax.psum(own_rows, axis_name=across), axis_name=axis_tag)  136 us
    all_gather x1, waiting for transfers between devices, on_device(): lax.all_gather(w_in, ('dp', 'rep'), axis=0, tiled=True)  114 us
    all_gather x1, waiting for transfers between devices, on_device(): lax.all_gather(w_out, ('dp', 'rep'), axis=0, tiled=True)  111 us
    psum x1, blocking collectives, on_device(): lax.psum(jnp.sum(centred * centred * row_weight, axis=0), ('dp', 'rep'))  72.7 us
    reduce_sum x1, other arithmetic, on_device(): jnp.sum(convolved * row_weight, axis=0)  38.3 us
    unnamed x14, local copies, waits for them, and re-layouts  22.6 us
    dot_general x1, matrix products, project_in(): return jnp.dot(normed, weight_rows, preferred_element_type=jnp.float32)  11.3 us
  transfers between devices with their start and end apart: 2, of which 2 were waited for; matrix products, arithmetic and copies ran while one was open for 4% of the time, Pallas kernels for 0%

profile of v1, /device:TPU:1, one launch (start us, length us, event | category | flops | bytes accessed | tf_op | source)
XLA Modules:
  0.0 548.5 jit_solution(2764939833308996390)
XLA Ops:
  6.5 0.7 all-gather.7.cloned.1.call-update
  7.3 0.7 all-gather.5.cloned.1.call-update
  8.0 1.3 reduce_sum.54
  9.3 0.8 reduce-window.8
  10.1 0.6 iota_compare_fusion.1
  10.8 0.7 fusion.26
  11.5 1.5 slice_reduce_fusion.29
  13.0 1.8 slice_reduce_fusion.30
  14.9 2.2 convert_reduce_fusion
  17.2 2.6 fusion.4
  19.8 0.1 slice_compare_fusion.29
  19.9 0.1 slice_compare_fusion.28
  20.1 111.2 %all-gather.7.cloned.1.call-done = bf16[256,6,1536]{2,1,0:T(8,128)(2,1)} async-done(((bf16[1,6,1536]{2,1,0:T(8,128)(2,1)}), bf16[256,6,1536]{2,1,0:T(8,128)(2,1)}) %all-gather.7.cloned.1.call-update) | async-done | bytes 4718608 | tf_op jit(solution)/shard_map/all_gather | solution.py:57
  131.3 8.5 %reshape.87 = bf16[1536,1536]{1,0:T(8,128)(2,1)} reshape(bf16[256,6,1536]{2,1,0:T(8,128)(2,1)} %all-gather.7.cloned.1.call-done) | data formatting | bytes 9437184
  139.8 113.5 %all-gather.5.cloned.1.call-done = bf16[256,6,3072]{2,1,0:T(8,128)(2,1)} async-done(((bf16[1,6,3072]{2,1,0:T(8,128)(2,1)}), bf16[256,6,3072]{2,1,0:T(8,128)(2,1)}) %all-gather.5.cloned.1.call-update) | async-done | bytes 9437200 | tf_op jit(solution)/shard_map/all_gather | solution.py:56
  253.3 14.2 %reshape.85 = bf16[1536,3072]{1,0:T(8,128)(2,1)} reshape(bf16[256,6,3072]{2,1,0:T(8,128)(2,1)} %all-gather.5.cloned.1.call-done) | data formatting | bytes 18874368
  267.5 11.3 %fusion.16 = f32[896,3072]{1,0:T(8,128)S(1)} fusion(bf16[1536,3072]{1,0:T(8,128)(2,1)} %reshape.85, bf16[1,896,1536]{2,1,0:T(8,128)(2,1)S(1)} %copy-done, f32[1536]{0:T(1024)S(1)} %copy-done.2, f32[1536]{0:T(1024)S(1)} %copy-done.3, f32[896]{0:T(1024)S(1)} %add_rsqrt_fusion.1, f32[896]{0:T(1024)S(1)} %broadcast_multiply_fusion.1), kind=kOutput, calls=%fused_computation.23 | convolution fusion | flops 8463974400 | bytes 23219200 | tf_op jit(solution)/shard_map/dot_general | solution.py:34
  278.8 1.5 fusion.13
  280.4 38.3 %multiply_reduce_fusion.1 = (f32[1536]{0:T(1024)S(1)}, f32[896,1536]{1,0:T(8,128)}) fusion(f32[896]{0:T(1024)S(1)} %fusion.26, f32[1536]{0:T(1024)S(1)} %get-tuple-element.34, pred[896]{0:T(1024)(128)(4,1)S(1)} %get-tuple-element.67, f32[1536]{0:T(1024)S(1)} %get-tuple-element.35, pred[896]{0:T(1024)(128)(4,1)S(1)} %get-tuple-element.39, ...), kind=kLoop, calls=%fused_computation.18 | loop fusion | flops 170654208 | bytes 8484608 | tf_op jit(solution)/shard_map/reduce_sum | solution.py:69
  318.7 8.8 %psum.21 = f32[1536]{0:T(1024)S(1)} all-reduce(f32[1536]{0:T(1024)S(1)} %get-tuple-element.36), channel_id=1, replica_groups=mesh['dp'=64,'rep'=4] {'rep'}, use_global_device_ids=true, to_apply=%region_6.7 | all-reduce | flops 1536 | bytes 12288 | tf_op jit(solution)/shard_map/psum | solution.py:46
  327.5 127.7 %psum.22 = f32[1536]{0:T(1024)S(1)} all-reduce(f32[1536]{0:T(1024)S(1)} %psum.21), channel_id=1, replica_groups=mesh['dp'=64,'rep'=4] {'dp'}, use_global_device_ids=true, to_apply=%region_7.8 | all-reduce | flops 1536 | bytes 12288 | tf_op jit(solution)/shard_map/psum | solution.py:46
  455.2 3.3 multiply_reduce_fusion
  458.5 72.7 %psum.23 = f32[1536]{0:T(1024)S(1)} all-reduce(f32[1536]{0:T(1024)S(1)} %multiply_reduce_fusion), channel_id=1, replica_groups=mesh['dp'=64,'rep'=4] {'dp','rep'}, use_global_device_ids=true, to_apply=%region_9.10 | all-reduce | flops 1536 | bytes 12288 | tf_op jit(solution)/shard_map/psum | solution.py:72
  531.2 10.5 %fusion.15 = bf16[1,896,1536]{2,1,0:T(8,128)(2,1)} fusion(bf16[1536,1536]{1,0:T(8,128)(2,1)} %reshape.87, bf16[1,896,1536]{2,1,0:T(8,128)(2,1)S(1)} %copy-done.1, f32[896,1536]{1,0:T(8,128)} %get-tuple-element.37, f32[1536]{0:T(1024)S(1)} %copy-done.4, f32[1536]{0:T(1024)S(1)} %copy-done.5, f32[1536]{0:T(1024)S(1)} %add_rsqrt_fusion, ...), kind=kOutput, calls=%fused_computation.22 | convolution fusion | flops 4245749760 | bytes 15754112 | tf_op jit(solution)/shard_map/dot_general | solution.py:38
  (21 shorter events, 0.3 us)
Async XLA Ops:
  6.5 124.8 %all-gather.7.cloned.1.call-start = ((), (), s32[]{:S(2)}) async-start(), calls=%async_computation.1 | async-start | bytes 6316032 | tf_op jit(solution)/shard_map/all_gather | solution.py:57
  7.3 246.1 %all-gather.5.cloned.1.call-start = ((), (), s32[]{:S(2)}) async-start(), calls=%async_computation | async-start | bytes 12632064 | tf_op jit(solution)/shard_map/all_gather | solution.py:56
  139.8 127.7 %copy-start = (bf16[1,896,1536]{2,1,0:T(8,128)(2,1)S(1)}, bf16[1,896,1536]{2,1,0:T(8,128)(2,1)}, u32[]{:S(2)}) copy-start(bf16[1,896,1536]{2,1,0:T(8,128)(2,1)} %param.9) | copy-start | bytes 8257540
  139.8 127.7 %copy-start.2 = (f32[1536]{0:T(1024)S(1)}, f32[1536]{0:T(1024)}, u32[]{:S(2)}) copy-start(f32[1536]{0:T(1024)} %param.12) | copy-start | bytes 18436
  139.8 127.7 %copy-start.3 = (f32[1536]{0:T(1024)S(1)}, f32[1536]{0:T(1024)}, u32[]{:S(2)}) copy-start(f32[1536]{0:T(1024)} %param.11) | copy-start | bytes 18436
  280.4 250.9 %copy-start.4 = (f32[1536]{0:T(1024)S(1)}, f32[1536]{0:T(1024)}, u32[]{:S(2)}) copy-start(f32[1536]{0:T(1024)} %param.16) | copy-start | bytes 18436
  280.4 250.8 %copy-start.5 = (f32[1536]{0:T(1024)S(1)}, f32[1536]{0:T(1024)}, u32[]{:S(2)}) copy-start(f32[1536]{0:T(1024)} %param.15) | copy-start | bytes 18436
  318.7 212.5 %copy-start.1 = (bf16[1,896,1536]{2,1,0:T(8,128)(2,1)S(1)}, bf16[1,896,1536]{2,1,0:T(8,128)(2,1)}, u32[]{:S(2)}) copy-start(bf16[1,896,1536]{2,1,0:T(8,128)(2,1)} %param.9) | copy-start | bytes 8257540
Sparse Core Ops, SparseCore 0:
  11.2 120.0 all-gather.6
  135.1 118.1 all-gather.4
